TPU v7x, 128 devices: a whole 4x4x4 slice. The times are simulated.
128 devices in a mesh: rows: 8 (over z, core), cols: 16 (over y, x).
Axes of the slice: x: 4, y: 4, z: 4, core: 2. Of those that a mesh axis runs over, the one named last changes fastest.
Arguments:
- model_dir: float32 [131072, 128], P('cols'), may hold values from -6 to 6
- sens_blocks: bfloat16 [8, 6144, 128, 128], P('rows', 'cols'), may hold values from -0.0625 to 0.0625
- blk_row: int32 [8, 6144], P('rows', 'cols'), may hold values from 0 to 31, as said below
- blk_col: int32 [8, 6144], P('rows', 'cols'), may hold values from 0 to 63, as said below
- blk_count: int32 [8, 16], P('rows', 'cols'), may hold values from 48 to 384, as said below
- send_order: int32 [16, 64], P('cols'), may hold values from 0 to 63, each once within a row
- neighbors: int32 [4, 131072], P(None, 'cols'), may hold values from 0 to 131071, as said below
- face_weight: float32 [4, 131072], P(None, 'cols'), may hold values from 0.05 to 0.5
Outputs:
- data_image: float32 [32768, 128], P('rows')
- normal_product: float32 [131072, 128], P('cols')
Inputs may be any that keep to these rules, and one draw needn't show every extreme that they name: Within one device's 384 slots the pairs (blk_row, blk_col) are all different. `blk_col`: paired with blk_row as stated there. The live slots of a device are its first blk_count slots; some device has all 384 live. `send_order`: each row is a permutation. `neighbors`: every neighbour lies within 64 of the cell's own number.
All inputs are finite; a program needn't handle non-finite values.
Results may differ from a plain program's by a relative error of at most 0.0029.
Values may be sent and summed in bfloat16 or wider, within the bound.
A program may use at most 192 MiB of HBM per device.

v0:
```python
import math
import jax
import jax.numpy as jnp
from jax import lax
from jax.sharding import PartitionSpec as P

BLK = 128
RB_DEV = 32
RIM = 64


def padded_2(block, sides, width):
    for axis, dim in sides:
        count = lax.axis_size(axis)
        forward = [(i, i + 1) for i in range(count - 1)]
        backward = [(target, source) for source, target in forward]
        low = lax.ppermute(
            lax.slice_in_dim(block, block.shape[dim] - width, None, axis=dim), axis, forward
        )
        high = lax.ppermute(lax.slice_in_dim(block, 0, width, axis=dim), axis, backward)
        block = jnp.concatenate([low, block, high], axis=dim)
    return block


def haar_matrix(order_n):
    matrix = jnp.ones((1, 1), jnp.float32)
    factor = 1.0 / math.sqrt(2.0)
    while matrix.shape[0] < order_n:
        length = matrix.shape[0]
        upper_half = jnp.kron(matrix, jnp.array([[1.0, 1.0]], jnp.float32))
        lower_half = jnp.kron(
            jnp.eye(length, dtype=jnp.float32), jnp.array([[1.0, -1.0]], jnp.float32)
        )
        matrix = jnp.concatenate([upper_half, lower_half], axis=0) * factor
    return matrix


def one_hot(indices, length, dtype):
    return (indices[:, None] == lax.iota(jnp.int32, length)[None, :]).astype(dtype)


def smoothing(extended, center, neighbors, face_weight, offset):
    cell_count, width = center.shape
    tile_count = cell_count // BLK
    tiles = extended.reshape(tile_count + 1, BLK, width)
    window = jnp.concatenate([tiles[:-1], tiles[1:]], axis=1)
    starts = lax.iota(jnp.int32, tile_count) * BLK
    local_index = (neighbors - offset).reshape(4, tile_count, BLK) - starts[None, :, None]
    span = lax.iota(jnp.int32, 2 * BLK)
    weights = jnp.zeros((tile_count, BLK, 2 * BLK), jnp.float32)
    for face in range(4):
        face_w = face_weight[face].reshape(tile_count, BLK)
        weights = weights + jnp.where(
            local_index[face][:, :, None] == span[None, None, :], face_w[:, :, None], 0.0
        )
    mixed = jnp.einsum("bij,bjn->bin", weights, window, precision=lax.Precision.HIGHEST)
    total_w = jnp.sum(face_weight, axis=0)
    return total_w[:, None] * center - mixed.reshape(cell_count, width)


def synthesize(haar_basis, returned, send_onehot, block_count, cell_count):
    share_cols = returned.shape[-1]
    flat_back = returned.reshape(block_count, BLK * share_cols)
    cell_side = jnp.einsum("jb,jm->bm", send_onehot, flat_back, precision=lax.Precision.HIGHEST)
    cell_side = cell_side.reshape(block_count, BLK, share_cols)
    result = jnp.einsum("ji,bjn->bin", haar_basis, cell_side, precision=lax.Precision.HIGHEST)
    return result.reshape(cell_count, share_cols)


def local(model_dir, sens_blocks, blk_row, blk_col, blk_count, send_order, neighbors, face_weight):
    highest = lax.Precision.HIGHEST
    cell_count, vec_width = model_dir.shape
    block_count = cell_count // BLK
    col_devices = lax.axis_size("cols")
    per_peer = block_count // col_devices
    haar_basis = jnp.asarray(haar_matrix(BLK), jnp.float32)
    cell_blocks = model_dir.reshape(block_count, BLK, vec_width)
    coeffs = jnp.einsum("ij,bjn->bin", haar_basis, cell_blocks, precision=highest).astype(
        jnp.bfloat16
    )
    order_here = send_order[0]
    send_half = one_hot(order_here, block_count, jnp.bfloat16)
    ordered = jnp.dot(
        send_half, coeffs.reshape(block_count, BLK * vec_width), preferred_element_type=jnp.float32
    )
    outgoing = ordered.astype(jnp.bfloat16).reshape(col_devices, per_peer * BLK, vec_width)
    wavelet = lax.all_to_all(outgoing, "cols", split_axis=0, concat_axis=0, tiled=True).reshape(
        block_count, BLK * vec_width
    )
    rows_here = blk_row[0]
    cols_here = blk_col[0]
    sensors = sens_blocks[0]
    slot_count = sensors.shape[0]
    live_slot = lax.iota(jnp.int32, slot_count) < blk_count[0, 0]
    pick_cols = one_hot(cols_here, block_count, jnp.bfloat16)
    picked = jnp.dot(pick_cols, wavelet, preferred_element_type=jnp.float32).astype(jnp.bfloat16)
    picked = picked.reshape(slot_count, BLK, vec_width)
    forward = jnp.einsum("kij,kjn->kin", sensors, picked, preferred_element_type=jnp.float32)
    row_mask = (one_hot(rows_here, RB_DEV, jnp.float32) * live_slot[:, None].astype(jnp.float32)).T
    partial_rows = jnp.dot(
        row_mask, forward.reshape(slot_count, BLK * vec_width), precision=highest
    )
    partial_rows = partial_rows.reshape(RB_DEV, BLK, vec_width)
    predicted = lax.psum(partial_rows, "cols")
    data_image = predicted.reshape(RB_DEV * BLK, vec_width)
    image_half = predicted.astype(jnp.bfloat16).reshape(RB_DEV, BLK * vec_width)
    pick_rows = one_hot(rows_here, RB_DEV, jnp.bfloat16)
    chosen = jnp.dot(pick_rows, image_half, preferred_element_type=jnp.float32).astype(jnp.bfloat16)
    chosen = chosen.reshape(slot_count, BLK, vec_width)
    adjoint = jnp.einsum("kij,kin->kjn", sensors, chosen, preferred_element_type=jnp.float32)
    col_mask = (
        one_hot(cols_here, block_count, jnp.float32) * live_slot[:, None].astype(jnp.float32)
    ).T
    partial_cols = jnp.dot(
        col_mask, adjoint.reshape(slot_count, BLK * vec_width), precision=highest
    )
    partial_cols = partial_cols.reshape(block_count, BLK, vec_width)
    extended = padded_2(model_dir, (("cols", 0),), RIM)
    offset = lax.axis_index("cols") * cell_count - RIM
    send_full = one_hot(order_here, block_count, jnp.float32)
    summed = lax.psum(partial_cols, "rows")
    returned = lax.all_to_all(
        summed.reshape(col_devices, per_peer * BLK, vec_width),
        "cols",
        split_axis=0,
        concat_axis=0,
        tiled=True,
    )
    synthesis = synthesize(haar_basis, returned, send_full, block_count, cell_count)
    normal_product = synthesis + smoothing(extended, model_dir, neighbors, face_weight, offset)
    return (data_image, normal_product)


def solution(mesh):
    placed = (
        P("cols", None),
        P("rows", "cols", None, None),
        P("rows", "cols"),
        P("rows", "cols"),
        P("rows", "cols"),
        P("cols", None),
        P(None, "cols"),
        P(None, "cols"),
    )
    return jax.shard_map(
        local,
        mesh=mesh,
        in_specs=placed,
        out_specs=(P("rows", None), P("cols", None)),
        check_vma=False,
    )
```

profile of v0, /device:TPU:65, one launch (start us, length us, event | category | flops | bytes accessed | tf_op | source)
XLA Modules:
  0.0 500.2 jit_solution(12547211673845322062)
XLA Ops:
  7.3 0.7 mul.557
  8.0 0.1 mul.558
  8.2 0.7 mul.541
  8.8 0.1 mul.542
  8.9 0.7 mul.525
  9.6 0.1 mul.526
  9.7 0.7 mul.509
  10.4 0.7 mul.493
  11.1 0.1 mul.494
  11.2 0.1 mul.476
  11.3 0.7 mul.478
  12.0 0.1 mul.479
  12.1 0.7 mul.468
  12.9 0.1 copy.29
  13.8 6.0 %convolution_convert_fusion.3 = bf16[128,64,128]{2,0,1:T(8,128)(2,1)S(1)} fusion(f32[64,128,128]{2,1,0:T(8,128)} %bitcast.118, f32[64,128]{1,0:T(8,128)S(1)} %broadcast_multiply_fusion, f32[64,128]{1,0:T(8,128)S(1)} %copy.31), kind=kOutput, calls=%fused_computation.50 | convolution fusion | flops 1611694080 | bytes 6356992 | tf_op jit(solution)/shard_map/ij,bjn->bin/dot_general | solution.py:78
  19.9 1.7 convolution_convert_fusion.2
  21.6 2.3 reshape.406
  23.9 6.8 %all-to-all-start = ((bf16[16,512,128]{2,1,0:T(8,128)(2,1)}), bf16[16,512,128]{2,1,0:T(8,128)(2,1)S(1)}, u32[]{:S(2)}, u32[]{:S(2)}) async-start(bf16[16,512,128]{2,1,0:T(8,128)(2,1)} %reshape.406), calls=%async_computation | async-start | bytes 4194304 | tf_op jit(solution)/shard_map/all_to_all | solution.py:87
  30.7 0.5 all-reduce.3.cloned.1.call-start
  31.9 29.3 %all-to-all-done = bf16[16,512,128]{2,1,0:T(8,128)(2,1)S(1)} async-done(((bf16[16,512,128]{2,1,0:T(8,128)(2,1)}), bf16[16,512,128]{2,1,0:T(8,128)(2,1)S(1)}, u32[]{:S(2)}, u32[]{:S(2)}) %all-to-all-start) | async-done | bytes 2097184 | tf_op jit(solution)/shard_map/all_to_all | solution.py:87
  61.2 2.3 reshape.407
  63.4 5.1 %fusion.25 = bf16[48,8,128,128]{3,1,2,0:T(8,128)(2,1)S(1)} fusion(bf16[64,16384]{1,0:T(8,128)(2,1)} %reshape.407, s32[384]{0:T(512)S(1)} %reduce.1), kind=kOutput, calls=%fused_computation.28 | convolution fusion | flops 811622400 | bytes 14681600 | tf_op jit(solution)/shard_map/dot_general | solution.py:96
  68.5 6.5 %copy.49 = bf16[48,8,128,128]{3,2,1,0:T(8,128)(2,1)} copy(bf16[48,8,128,128]{3,1,2,0:T(8,128)(2,1)S(1)} %fusion.25) | data formatting | bytes 25165824
  75.0 22.1 %fusion.8 = f32[384,128,128]{1,2,0:T(8,128)} fusion(bf16[384,128,128]{2,1,0:T(8,128)(2,1)} %bitcast.116, bf16[1,384,128,128]{3,2,1,0:T(8,128)(2,1)} %param.23), kind=kOutput, calls=%fused_computation.11 | convolution fusion | flops 1610612736 | bytes 50331648 | tf_op jit(solution)/shard_map/kij,kjn->kin/dot_general | solution.py:98
  97.1 25.0 %copy.33 = f32[384,128,128]{0,2,1:T(8,128)} copy(f32[384,128,128]{1,2,0:T(8,128)} %fusion.8) | data formatting | bytes 50331648 | tf_op jit(solution)/shard_map/kij,kjn->kin/dot_general | solution.py:98
  122.1 27.2 %fusion.2 = f32[32,128,128]{2,0,1:T(8,128)} fusion(f32[384,128,128]{0,2,1:T(8,128)} %copy.33, f32[384]{0:T(512)S(1)} %fusion.70, s32[384]{0:T(512)S(1)} %reduce), kind=kOutput, calls=%fused_computation.2 | convolution fusion | flops 2415943680 | bytes 27266048 | tf_op jit(solution)/shard_map/dot_general | solution.py:100
  149.4 88.7 %all-reduce.3.cloned.1.call-done = f32[32,128,128]{2,0,1:T(8,128)} async-done(((f32[32,128,128]{2,0,1:T(8,128)}), f32[32,128,128]{2,0,1:T(8,128)}) %all-reduce.3.cloned.1.call-update) | async-done | bytes 2097168 | tf_op jit(solution)/shard_map/psum | solution.py:104
  238.1 9.7 %fusion.26 = bf16[48,8,128,128]{3,1,2,0:T(8,128)(2,1)} fusion(s32[384]{0:T(512)S(1)} %reduce, f32[32,128,128]{2,0,1:T(8,128)} %all-reduce.3.cloned.1.call-done), kind=kOutput, calls=%fused_computation.29 | convolution fusion | flops 409481216 | bytes 14681600 | tf_op jit(solution)/shard_map/dot_general | solution.py:108
  247.8 12.0 %copy.50 = bf16[48,8,128,128]{3,2,1,0:T(8,128)(2,1)} copy(bf16[48,8,128,128]{3,1,2,0:T(8,128)(2,1)} %fusion.26) | data formatting | bytes 25165824
  259.8 13.2 %fusion.11 = f32[384,128,128]{1,2,0:T(8,128)} fusion(bf16[384,128,128]{2,1,0:T(8,128)(2,1)} %bitcast.117, bf16[1,384,128,128]{3,2,1,0:T(8,128)(2,1)S(1)} %bitcast.115), kind=kOutput, calls=%fused_computation.12 | convolution fusion | flops 1610612736 | bytes 50331648 | tf_op jit(solution)/shard_map/kij,kin->kjn/dot_general | solution.py:110
  273.0 25.0 %copy.37 = f32[384,128,128]{0,2,1:T(8,128)} copy(f32[384,128,128]{1,2,0:T(8,128)} %fusion.11) | data formatting | bytes 50331648 | tf_op jit(solution)/shard_map/kij,kin->kjn/dot_general | solution.py:110
  298.0 27.9 %fusion = f32[64,128,128]{2,0,1:T(8,128)S(1)} fusion(f32[384,128,128]{0,2,1:T(8,128)} %copy.37, f32[384]{0:T(512)S(1)} %fusion.70, s32[384]{0:T(512)S(1)} %reduce.1), kind=kOutput, calls=%fused_computation | convolution fusion | flops 4831887360 | bytes 29363200 | tf_op jit(solution)/shard_map/dot_general | solution.py:114
  325.9 4.4 copy.38
  330.3 0.8 fusion.80
  331.1 2.5 collective-permute-start
  333.7 1.3 collective-permute-start.1
  335.1 65.8 %all-reduce.5.cloned.1.call-done = f32[16,512,128]{2,1,0:T(8,128)} async-done(((f32[16,512,128]{2,1,0:T(8,128)}), f32[16,512,128]{2,1,0:T(8,128)}) %all-reduce.5.cloned.1.call-update) | async-done | bytes 4194320 | tf_op jit(solution)/shard_map/psum | solution.py:121
  400.9 6.8 %all-to-all-start.1 = ((f32[16,512,128]{2,1,0:T(8,128)}), f32[16,512,128]{2,1,0:T(8,128)}, u32[]{:S(2)}, u32[]{:S(2)}) async-start(f32[16,512,128]{2,1,0:T(8,128)} %all-reduce.5.cloned.1.call-done), calls=%async_computation.1 | async-start | bytes 8388608 | tf_op jit(solution)/shard_map/all_to_all | solution.py:122
  407.7 0.1 fusion.81
  408.0 4.0 pad_maximum_fusion.1
  412.0 3.8 fusion.93
  415.7 20.2 %fusion.14 = f32[64,128,128]{2,1,0:T(8,128)} fusion(f32[64,128]{1,0:T(8,128)S(1)} %bitcast.134, s32[64,128]{1,0:T(8,128)S(1)} %get-tuple-element.7, f32[64,128]{1,0:T(8,128)S(1)} %bitcast.135, s32[64,128]{1,0:T(8,128)S(1)} %get-tuple-element.8, f32[64,128]{1,0:T(8,128)S(1)} %bitcast.133, s32[64,128]{1,0:T(8,128)S(1)} %get-tuple-element.9, ...), kind=kOutput, calls=%fused_computation.13 | convolution fusion | flops 3244294144 | bytes 12845056 | tf_op jit(solution)/shard_map/bij,bjn->bin/dot_general | solution.py:56
  435.9 2.5 copy.34
  438.4 34.3 %all-to-all-done.1 = f32[16,512,128]{2,1,0:T(8,128)} async-done(((f32[16,512,128]{2,1,0:T(8,128)}), f32[16,512,128]{2,1,0:T(8,128)}, u32[]{:S(2)}, u32[]{:S(2)}) %all-to-all-start.1) | async-done | bytes 4194336 | tf_op jit(solution)/shard_map/all_to_all | solution.py:122
  472.7 4.9 reshape.415
  477.6 4.6 fusion.27
  482.3 6.3 %fusion.30 = f32[64,128,128]{1,2,0:T(8,128)S(1)} fusion(f32[64,128,128]{2,0,1:T(8,128)S(1)} %fusion.27, f32[64,128]{1,0:T(8,128)S(1)} %broadcast_multiply_fusion, f32[64,128]{1,0:T(8,128)S(1)} %copy.31), kind=kOutput, calls=%fused_computation.37 | convolution fusion | flops 1610645504 | bytes 8454144 | tf_op jit(solution)/shard_map/ji,bjn->bin/dot_general | solution.py:66
  488.6 4.6 bitcast_add_fusion
  (68 shorter events, 1.5 us)
Async XLA Ops:
  7.2 12.7 %copy-start.5 = (s32[1,64]{1,0:T(1,128)S(1)}, s32[1,64]{1,0:T(1,128)}, u32[]{:S(2)}) copy-start(s32[1,64]{1,0:T(1,128)} %param.27) | copy-start | bytes 772
  21.6 10.3 %copy-start.6 = (s32[1,384]{1,0:T(1,128)S(1)}, s32[1,384]{1,0:T(1,128)}, u32[]{:S(2)}) copy-start(s32[1,384]{1,0:T(1,128)} %param.25) | copy-start | bytes 4612
  21.6 10.3 %copy-start.7 = (s32[1,384]{1,0:T(1,128)S(1)}, s32[1,384]{1,0:T(1,128)}, u32[]{:S(2)}) copy-start(s32[1,384]{1,0:T(1,128)} %param.24) | copy-start | bytes 4612
  23.9 37.3 %all-to-all-start = ((bf16[16,512,128]{2,1,0:T(8,128)(2,1)}), bf16[16,512,128]{2,1,0:T(8,128)(2,1)S(1)}, u32[]{:S(2)}, u32[]{:S(2)}) async-start(bf16[16,512,128]{2,1,0:T(8,128)(2,1)} %reshape.406), calls=%async_computation | async-start | bytes 4194304 | tf_op jit(solution)/shard_map/all_to_all | solution.py:87
  30.7 207.4 %all-reduce.3.cloned.1.call-start = ((), (), s32[]{:S(2)}) async-start(), calls=%async_computation.2 | async-start | bytes 4194304 | tf_op jit(solution)/shard_map/psum | solution.py:104
  149.3 251.6 %all-reduce.5.cloned.1.call-start = ((), (), s32[]{:S(2)}) async-start(), calls=%async_computation.3 | async-start | bytes 8388608 | tf_op jit(solution)/shard_map/psum | solution.py:121
  238.1 21.7 %slice-start = ((s8[12582912]{0:T(1024)(128)(4,1)}), s8[4194304]{0:T(1024)(128)(4,1)S(1)}, s32[]{:S(2)}) async-start(s8[12582912]{0:T(1024)(128)(4,1)} %bitcast.114), calls=%async_computation.4 | async-start | bytes 8388608
  238.1 21.7 %slice-start.1 = ((s8[12582912]{0:T(1024)(128)(4,1)}), s8[4194304]{0:T(1024)(128)(4,1)S(1)}, s32[]{:S(2)}) async-start(s8[12582912]{0:T(1024)(128)(4,1)} %bitcast.114), calls=%async_computation.5 | async-start | bytes 8388608
  247.8 12.0 %slice-start.2 = ((s8[12582912]{0:T(1024)(128)(4,1)}), s8[4194304]{0:T(1024)(128)(4,1)S(1)}, s32[]{:S(2)}) async-start(s8[12582912]{0:T(1024)(128)(4,1)} %bitcast.114), calls=%async_computation.6 | async-start | bytes 8388608
  330.3 4.7 copy-start.4
  331.1 76.8 %collective-permute-start = (f32[64,128]{1,0:T(8,128)S(1)}, f32[64,128]{1,0:T(8,128)S(1)}, u32[]{:S(2)}, u32[]{:S(2)}) collective-permute-start(f32[64,128]{1,0:T(8,128)S(1)} %get-tuple-element.4), channel_id=1, source_target_pairs={{0,1},{1,2},{2,3},{3,4},{4,5},{5,6},{6,7},{7,8},{8,9},{9,10},{10,1... | collective-permute-start | bytes 98312 | tf_op jit(solution)/shard_map/ppermute | solution.py:17
  333.7 74.3 %collective-permute-start.1 = (f32[64,128]{1,0:T(8,128)S(1)}, f32[64,128]{1,0:T(8,128)S(1)}, u32[]{:S(2)}, u32[]{:S(2)}) collective-permute-start(f32[64,128]{1,0:T(8,128)S(1)} %get-tuple-element.5), channel_id=1, source_target_pairs={{1,0},{2,1},{3,2},{4,3},{5,4},{6,5},{7,6},{8,7},{9,8},{10,9},{11,1... | collective-permute-start | bytes 98312 | tf_op jit(solution)/shard_map/ppermute | solution.py:20
  335.1 72.6 %copy-start.3 = (f32[4,8192]{1,0:T(4,128)S(1)}, f32[4,8192]{1,0:T(4,128)}, u32[]{:S(2)}) copy-start(f32[4,8192]{1,0:T(4,128)} %param.29) | copy-start | bytes 393220
  400.9 71.8 %all-to-all-start.1 = ((f32[16,512,128]{2,1,0:T(8,128)}), f32[16,512,128]{2,1,0:T(8,128)}, u32[]{:S(2)}, u32[]{:S(2)}) async-start(f32[16,512,128]{2,1,0:T(8,128)} %all-reduce.5.cloned.1.call-done), calls=%async_computation.1 | async-start | bytes 8388608 | tf_op jit(solution)/shard_map/all_to_all | solution.py:122
  415.7 20.2 %copy-start.1 = (f32[32,128,128]{2,0,1:T(8,128)S(1)}, f32[32,128,128]{2,0,1:T(8,128)}, u32[]{:S(2)}) copy-start(f32[32,128,128]{2,0,1:T(8,128)} %all-reduce.3.cloned.1.call-done) | copy-start | bytes 6291460
  482.3 6.3 %copy-start = (f32[8192,128]{1,0:T(8,128)S(1)}, f32[8192,128]{1,0:T(8,128)}, u32[]{:S(2)}) copy-start(f32[8192,128]{1,0:T(8,128)} %param.22) | copy-start | bytes 12582916
  482.3 6.3 %copy-start.2 = (f32[64,128,128]{2,1,0:T(8,128)S(1)}, f32[64,128,128]{2,1,0:T(8,128)}, u32[]{:S(2)}) copy-start(f32[64,128,128]{2,1,0:T(8,128)} %fusion.14) | copy-start | bytes 12582916
Sparse Core Ops, SparseCore 0:
  149.4 88.5 all-reduce.2
  330.4 70.4 all-reduce.4
where the time goes:
time: 507 us; the launch traced here: 500 us
  waiting for transfers between devices  218 us (43%)
  matrix products  144 us (28%)
  local copies, waits for them, and re-layouts  91.8 us (18%)
  starting transfers between devices  17.9 us (4%)
  between operations  15.3 us (3%)
  other arithmetic  13.2 us (3%)
    psum x1, waiting for transfers between devices, local(): predicted = lax.psum(partial_rows, 'cols')  88.7 us
    psum x1, waiting for transfers between devices, local(): summed = lax.psum(partial_cols, 'rows')  65.8 us
    all_to_all x1, waiting for transfers between devices, local(): lax.all_to_all(summed.reshape(col_devices, per_peer * BLK, vec_width), 'c...  34.3 us
    all_to_all x1, waiting for transfers between devices, local(): lax.all_to_all(outgoing, 'cols', split_axis=0, concat_axis=0, tiled=True)  29.3 us
    dot_general x1, matrix products, local(): jnp.dot(col_mask, adjoint.reshape(slot_count, BLK * vec_width), precision...  27.9 us
    dot_general x1, matrix products, local(): jnp.dot(row_mask, forward.reshape(slot_count, BLK * vec_width), precision...  27.2 us
    dot_general x1, local copies, waits for them, and re-layouts, local(): jnp.einsum('kij,kin->kjn', sensors, chosen, preferred_element_type=jnp.fl...  25 us
    dot_general x1, local copies, waits for them, and re-layouts, local(): jnp.einsum('kij,kjn->kin', sensors, picked, preferred_element_type=jnp.fl...  25 us
  transfers between devices with their start and end apart: 6, of which 4 were waited for; matrix products, arithmetic and copies ran while one was open for 6% of the time, Pallas kernels for 0%

commit v1 on v0

--- a/solution.py
+++ b/solution.py
@@ -7,6 +7,17 @@
 BLK = 128
 RB_DEV = 32
 RIM = 64
+
+
+def drive_gates(u_in):
+    mesh_name = "cols"
+    n_dev_all = lax.axis_size(mesh_name)
+    current_block = u_in
+    for no in [dev_i for dev_i in (1, 2, 4, 8, 16) if dev_i < n_dev_all]:
+        current_block = current_block + lax.ppermute(
+            current_block, mesh_name, tuple(((src_i, src_i ^ no) for src_i in range(n_dev_all)))
+        )
+    return current_block
 
 
 def padded_2(block, sides, width):
@@ -101,7 +112,7 @@
         row_mask, forward.reshape(slot_count, BLK * vec_width), precision=highest
     )
     partial_rows = partial_rows.reshape(RB_DEV, BLK, vec_width)
-    predicted = lax.psum(partial_rows, "cols")
+    predicted = drive_gates(partial_rows)
     data_image = predicted.reshape(RB_DEV * BLK, vec_width)
     image_half = predicted.astype(jnp.bfloat16).reshape(RB_DEV, BLK * vec_width)
     pick_rows = one_hot(rows_here, RB_DEV, jnp.bfloat16)

time: 507 us -> 604 us (1.19)
  waiting for transfers between devices: 218 us -> 310 us
  starting transfers between devices: 17.9 us -> 24.2 us
    ppermute x0 -> x4, waiting for transfers between devices: none -> 174 us  [drive_gates(): lax.ppermute(current_block, mesh_name, tuple(((src_i, src_i ^ no) for src...]
    psum x1 -> x0, waiting for transfers between devices: 88.7 us -> none  [local(): predicted = lax.psum(partial_rows, 'cols')]
    ppermute x0 -> x4, starting transfers between devices: none -> 7.78 us  [drive_gates(): lax.ppermute(current_block, mesh_name, tuple(((src_i, src_i ^ no) for src...]
    psum x1, waiting for transfers between devices: 65.8 us -> 72.2 us  [local(): summed = lax.psum(partial_cols, 'rows')]
  transfers between devices with their start and end apart: 6 -> 9, of which waited for: 4 -> 7; matrix products, arithmetic and copies ran while one was open for 6% -> 5% of each run, Pallas kernels for 0% -> 0%
where the time goes in v1:
time: 604 us; the launch traced here: 598 us
  waiting for transfers between devices  310 us (51%)
  matrix products  140 us (23%)
  local copies, waits for them, and re-layouts  92 us (15%)
  starting transfers between devices  24.2 us (4%)
  other arithmetic  16.5 us (3%)
  between operations  15.4 us (3%)
    ppermute x4, waiting for transfers between devices, drive_gates(): lax.ppermute(current_block, mesh_name, tuple(((src_i, src_i ^ no) for src...  174 us
    psum x1, waiting for transfers between devices, local(): summed = lax.psum(partial_cols, 'rows')  72.2 us
    all_to_all x1, waiting for transfers between devices, local(): lax.all_to_all(summed.reshape(col_devices, per_peer * BLK, vec_width), 'c...  34.5 us
    all_to_all x1, waiting for transfers between devices, local(): lax.all_to_all(outgoing, 'cols', split_axis=0, concat_axis=0, tiled=True)  29.2 us
    dot_general x1, matrix products, local(): jnp.dot(col_mask, adjoint.reshape(slot_count, BLK * vec_width), precision...  28.1 us
    dot_general x1, matrix products, local(): jnp.dot(row_mask, forward.reshape(slot_count, BLK * vec_width), precision...  26.3 us
    dot_general x1, local copies, waits for them, and re-layouts, local(): jnp.einsum('kij,kin->kjn', sensors, chosen, preferred_element_type=jnp.fl...  24.9 us
    dot_general x1, local copies, waits for them, and re-layouts, local(): jnp.einsum('kij,kjn->kin', sensors, picked, preferred_element_type=jnp.fl...  24.9 us
  transfers between devices with their start and end apart: 9, of which 7 were waited for; matrix products, arithmetic and copies ran while one was open for 5% of the time, Pallas kernels for 0%

profile of v1, /device:TPU:65, one launch (start us, length us, event | category | flops | bytes accessed | tf_op | source)
XLA Modules:
  0.0 598.1 jit_solution(17836447287611784091)
XLA Ops:
  7.3 0.7 mul.557
  8.2 0.7 mul.541
  8.9 0.7 mul.525
  9.7 0.7 mul.509
  10.4 0.7 mul.493
  11.3 0.7 mul.478
  12.1 0.7 mul.468
  13.8 6.0 %convolution_convert_fusion.3 = bf16[128,64,128]{2,0,1:T(8,128)(2,1)S(1)} fusion(f32[64,128,128]{2,1,0:T(8,128)} %bitcast.116, f32[64,128]{1,0:T(8,128)S(1)} %broadcast_multiply_fusion, f32[64,128]{1,0:T(8,128)S(1)} %copy.31), kind=kOutput, calls=%fused_computation.50 | convolution fusion | flops 1611694080 | bytes 6356992 | tf_op jit(solution)/shard_map/ij,bjn->bin/dot_general | solution.py:89
  19.9 1.7 convolution_convert_fusion.2
  21.6 2.3 reshape.406
  23.9 6.7 %all-to-all-start = ((bf16[16,512,128]{2,1,0:T(8,128)(2,1)}), bf16[16,512,128]{2,1,0:T(8,128)(2,1)S(1)}, u32[]{:S(2)}, u32[]{:S(2)}) async-start(bf16[16,512,128]{2,1,0:T(8,128)(2,1)} %reshape.406), calls=%async_computation | async-start | bytes 4194304 | tf_op jit(solution)/shard_map/all_to_all | solution.py:98
  30.7 0.6 all-reduce.2.cloned.1.call-start
  32.0 29.2 %all-to-all-done = bf16[16,512,128]{2,1,0:T(8,128)(2,1)S(1)} async-done(((bf16[16,512,128]{2,1,0:T(8,128)(2,1)}), bf16[16,512,128]{2,1,0:T(8,128)(2,1)S(1)}, u32[]{:S(2)}, u32[]{:S(2)}) %all-to-all-start) | async-done | bytes 2097184 | tf_op jit(solution)/shard_map/all_to_all | solution.py:98
  61.2 2.3 reshape.407
  63.4 5.1 fusion.25
  68.5 6.6 %copy.49 = bf16[48,8,128,128]{3,2,1,0:T(8,128)(2,1)} copy(bf16[48,8,128,128]{3,1,2,0:T(8,128)(2,1)S(1)} %fusion.25) | data formatting | bytes 25165824
  75.1 22.1 %fusion.8 = f32[384,128,128]{1,2,0:T(8,128)} fusion(bf16[384,128,128]{2,1,0:T(8,128)(2,1)} %bitcast.114, bf16[1,384,128,128]{3,2,1,0:T(8,128)(2,1)} %param.23), kind=kOutput, calls=%fused_computation.11 | convolution fusion | flops 1610612736 | bytes 50331648 | tf_op jit(solution)/shard_map/kij,kjn->kin/dot_general | solution.py:109
  97.2 24.9 %copy.33 = f32[384,128,128]{0,2,1:T(8,128)} copy(f32[384,128,128]{1,2,0:T(8,128)} %fusion.8) | data formatting | bytes 50331648 | tf_op jit(solution)/shard_map/kij,kjn->kin/dot_general | solution.py:109
  122.1 26.3 %fusion.2 = f32[32,128,128]{2,0,1:T(8,128)S(1)} fusion(f32[384,128,128]{0,2,1:T(8,128)} %copy.33, f32[384]{0:T(512)S(1)} %fusion.70, s32[384]{0:T(512)S(1)} %reduce), kind=kOutput, calls=%fused_computation.2 | convolution fusion | flops 2415943680 | bytes 27266048 | tf_op jit(solution)/shard_map/dot_general | solution.py:111
  148.5 45.0 %collective-permute-done = f32[32,128,128]{2,0,1:T(8,128)S(1)} collective-permute-done((f32[32,128,128]{2,0,1:T(8,128)S(1)}, f32[32,128,128]{2,0,1:T(8,128)S(1)}, u32[]{:S(2)}, u32[]{:S(2)}) %collective-permute-start) | collective-permute-done | bytes 2097184 | tf_op jit(solution)/shard_map/ppermute | solution.py:17
  193.5 0.5 add.27
  194.0 2.7 collective-permute-start.1
  196.7 43.6 %collective-permute-done.1 = f32[32,128,128]{2,0,1:T(8,128)S(1)} collective-permute-done((f32[32,128,128]{2,0,1:T(8,128)S(1)}, f32[32,128,128]{2,0,1:T(8,128)S(1)}, u32[]{:S(2)}, u32[]{:S(2)}) %collective-permute-start.1) | collective-permute-done | bytes 2097184 | tf_op jit(solution)/shard_map/ppermute | solution.py:17
  240.8 1.5 collective-permute-start.2
  242.3 42.2 %collective-permute-done.2 = f32[32,128,128]{2,0,1:T(8,128)S(1)} collective-permute-done((f32[32,128,128]{2,0,1:T(8,128)S(1)}, f32[32,128,128]{2,0,1:T(8,128)S(1)}, u32[]{:S(2)}, u32[]{:S(2)}) %collective-permute-start.2) | collective-permute-done | bytes 2097184 | tf_op jit(solution)/shard_map/ppermute | solution.py:17
  285.0 3.5 collective-permute-start.3
  288.5 43.1 %collective-permute-done.3 = f32[32,128,128]{2,0,1:T(8,128)S(1)} collective-permute-done((f32[32,128,128]{2,0,1:T(8,128)S(1)}, f32[32,128,128]{2,0,1:T(8,128)S(1)}, u32[]{:S(2)}, u32[]{:S(2)}) %collective-permute-start.3) | collective-permute-done | bytes 2097184 | tf_op jit(solution)/shard_map/ppermute | solution.py:17
  331.6 1.8 convert_bitcast_fusion
  333.4 6.5 %fusion.26 = bf16[48,8,128,128]{3,1,2,0:T(8,128)(2,1)} fusion(bf16[128,4,8,128]{3,2,1,0:T(8,128)(2,1)S(1)} %get-tuple-element.2, s32[384]{0:T(512)S(1)} %reduce), kind=kOutput, calls=%fused_computation.29 | convolution fusion | flops 408956928 | bytes 13633024 | tf_op jit(solution)/shard_map/dot_general | solution.py:119
  339.9 12.0 %copy.50 = bf16[48,8,128,128]{3,2,1,0:T(8,128)(2,1)} copy(bf16[48,8,128,128]{3,1,2,0:T(8,128)(2,1)} %fusion.26) | data formatting | bytes 25165824
  351.9 13.2 %fusion.11 = f32[384,128,128]{1,2,0:T(8,128)} fusion(bf16[384,128,128]{2,1,0:T(8,128)(2,1)} %bitcast.115, bf16[1,384,128,128]{3,2,1,0:T(8,128)(2,1)S(1)} %bitcast.113), kind=kOutput, calls=%fused_computation.12 | convolution fusion | flops 1610612736 | bytes 50331648 | tf_op jit(solution)/shard_map/kij,kin->kjn/dot_general | solution.py:121
  365.2 24.9 %copy.37 = f32[384,128,128]{0,2,1:T(8,128)} copy(f32[384,128,128]{1,2,0:T(8,128)} %fusion.11) | data formatting | bytes 50331648 | tf_op jit(solution)/shard_map/kij,kin->kjn/dot_general | solution.py:121
  390.1 28.1 %fusion = f32[64,128,128]{2,0,1:T(8,128)S(1)} fusion(f32[384,128,128]{0,2,1:T(8,128)} %copy.37, f32[384]{0:T(512)S(1)} %fusion.70, s32[384]{0:T(512)S(1)} %reduce.1), kind=kOutput, calls=%fused_computation | convolution fusion | flops 4831887360 | bytes 29363200 | tf_op jit(solution)/shard_map/dot_general | solution.py:125
  418.2 4.4 copy.38
  422.6 0.8 fusion.80
  423.5 1.3 collective-permute-start.4
  424.7 1.3 collective-permute-start.5
  426.2 72.2 %all-reduce.2.cloned.1.call-done = f32[16,512,128]{2,1,0:T(8,128)} async-done(((f32[16,512,128]{2,1,0:T(8,128)}), f32[16,512,128]{2,1,0:T(8,128)}) %all-reduce.2.cloned.1.call-update) | async-done | bytes 4194320 | tf_op jit(solution)/shard_map/psum | solution.py:132
  498.4 6.6 %all-to-all-start.1 = ((f32[16,512,128]{2,1,0:T(8,128)}), f32[16,512,128]{2,1,0:T(8,128)}, u32[]{:S(2)}, u32[]{:S(2)}) async-start(f32[16,512,128]{2,1,0:T(8,128)} %all-reduce.2.cloned.1.call-done), calls=%async_computation.1 | async-start | bytes 8388608 | tf_op jit(solution)/shard_map/all_to_all | solution.py:133
  505.3 4.0 pad_maximum_fusion.1
  509.2 3.8 fusion.93
  513.0 20.2 %fusion.14 = f32[64,128,128]{2,1,0:T(8,128)} fusion(f32[64,128]{1,0:T(8,128)S(1)} %bitcast.132, s32[64,128]{1,0:T(8,128)S(1)} %get-tuple-element.9, f32[64,128]{1,0:T(8,128)S(1)} %bitcast.133, s32[64,128]{1,0:T(8,128)S(1)} %get-tuple-element.10, f32[64,128]{1,0:T(8,128)S(1)} %bitcast.131, s32[64,128]{1,0:T(8,128)S(1)} %get-tuple-element.11, ...), kind=kOutput, calls=%fused_computation.13 | convolution fusion | flops 3244294144 | bytes 12845056 | tf_op jit(solution)/shard_map/bij,bjn->bin/dot_general | solution.py:67
  533.2 2.5 copy.34
  535.7 34.5 %all-to-all-done.1 = f32[16,512,128]{2,1,0:T(8,128)} async-done(((f32[16,512,128]{2,1,0:T(8,128)}), f32[16,512,128]{2,1,0:T(8,128)}, u32[]{:S(2)}, u32[]{:S(2)}) %all-to-all-start.1) | async-done | bytes 4194336 | tf_op jit(solution)/shard_map/all_to_all | solution.py:133
  570.2 5.2 reshape.415
  575.4 4.6 fusion.27
  580.0 6.3 %fusion.30 = f32[64,128,128]{1,2,0:T(8,128)S(1)} fusion(f32[64,128,128]{2,0,1:T(8,128)S(1)} %fusion.27, f32[64,128]{1,0:T(8,128)S(1)} %broadcast_multiply_fusion, f32[64,128]{1,0:T(8,128)S(1)} %copy.31), kind=kOutput, calls=%fused_computation.37 | convolution fusion | flops 1610645504 | bytes 8454144 | tf_op jit(solution)/shard_map/ji,bjn->bin/dot_general | solution.py:77
  586.4 4.6 bitcast_add_fusion
  (77 shorter events, 3.3 us)
Async XLA Ops:
  7.2 12.7 %copy-start.5 = (s32[1,64]{1,0:T(1,128)S(1)}, s32[1,64]{1,0:T(1,128)}, u32[]{:S(2)}) copy-start(s32[1,64]{1,0:T(1,128)} %param.27) | copy-start | bytes 772
  21.6 10.3 %copy-start.6 = (s32[1,384]{1,0:T(1,128)S(1)}, s32[1,384]{1,0:T(1,128)}, u32[]{:S(2)}) copy-start(s32[1,384]{1,0:T(1,128)} %param.25) | copy-start | bytes 4612
  21.6 10.4 %copy-start.7 = (s32[1,384]{1,0:T(1,128)S(1)}, s32[1,384]{1,0:T(1,128)}, u32[]{:S(2)}) copy-start(s32[1,384]{1,0:T(1,128)} %param.24) | copy-start | bytes 4612
  23.9 37.2 %all-to-all-start = ((bf16[16,512,128]{2,1,0:T(8,128)(2,1)}), bf16[16,512,128]{2,1,0:T(8,128)(2,1)S(1)}, u32[]{:S(2)}, u32[]{:S(2)}) async-start(bf16[16,512,128]{2,1,0:T(8,128)(2,1)} %reshape.406), calls=%async_computation | async-start | bytes 4194304 | tf_op jit(solution)/shard_map/all_to_all | solution.py:98
  30.7 467.8 %all-reduce.2.cloned.1.call-start = ((), (), s32[]{:S(2)}) async-start(), calls=%async_computation.2 | async-start | bytes 8388608 | tf_op jit(solution)/shard_map/psum | solution.py:132
  148.4 45.1 %collective-permute-start = (f32[32,128,128]{2,0,1:T(8,128)S(1)}, f32[32,128,128]{2,0,1:T(8,128)S(1)}, u32[]{:S(2)}, u32[]{:S(2)}) collective-permute-start(f32[32,128,128]{2,0,1:T(8,128)S(1)} %fusion.2), channel_id=1, source_target_pairs={{0,1},{1,0},{2,3},{3,2},{4,5},{5,4},{6,7},{7,6},{8,9},{9,8},{10,11... | collective-permute-start | bytes 6291464 | tf_op jit(solution)/shard_map/ppermute | solution.py:17
  194.0 46.3 %collective-permute-start.1 = (f32[32,128,128]{2,0,1:T(8,128)S(1)}, f32[32,128,128]{2,0,1:T(8,128)S(1)}, u32[]{:S(2)}, u32[]{:S(2)}) collective-permute-start(f32[32,128,128]{2,0,1:T(8,128)S(1)} %add.27), channel_id=1, source_target_pairs={{0,2},{1,3},{2,0},{3,1},{4,6},{5,7},{6,4},{7,5},{8,10},{9,11},{10,... | collective-permute-start | bytes 6291464 | tf_op jit(solution)/shard_map/ppermute | solution.py:17
  240.8 43.7 %collective-permute-start.2 = (f32[32,128,128]{2,0,1:T(8,128)S(1)}, f32[32,128,128]{2,0,1:T(8,128)S(1)}, u32[]{:S(2)}, u32[]{:S(2)}) collective-permute-start(f32[32,128,128]{2,0,1:T(8,128)S(1)} %add.28), channel_id=1, source_target_pairs={{0,4},{1,5},{2,6},{3,7},{4,0},{5,1},{6,2},{7,3},{8,12},{9,13},{10,... | collective-permute-start | bytes 6291464 | tf_op jit(solution)/shard_map/ppermute | solution.py:17
  285.0 46.6 %collective-permute-start.3 = (f32[32,128,128]{2,0,1:T(8,128)S(1)}, f32[32,128,128]{2,0,1:T(8,128)S(1)}, u32[]{:S(2)}, u32[]{:S(2)}) collective-permute-start(f32[32,128,128]{2,0,1:T(8,128)S(1)} %add.29), channel_id=1, source_target_pairs={{0,8},{1,9},{2,10},{3,11},{4,12},{5,13},{6,14},{7,15},{8,0},{9,1},... | collective-permute-start | bytes 6291464 | tf_op jit(solution)/shard_map/ppermute | solution.py:17
  333.4 18.5 %slice-start = ((s8[12582912]{0:T(1024)(128)(4,1)}), s8[4194304]{0:T(1024)(128)(4,1)S(1)}, s32[]{:S(2)}) async-start(s8[12582912]{0:T(1024)(128)(4,1)} %bitcast.112), calls=%async_computation.3 | async-start | bytes 8388608
  333.4 18.5 %slice-start.1 = ((s8[12582912]{0:T(1024)(128)(4,1)}), s8[4194304]{0:T(1024)(128)(4,1)S(1)}, s32[]{:S(2)}) async-start(s8[12582912]{0:T(1024)(128)(4,1)} %bitcast.112), calls=%async_computation.4 | async-start | bytes 8388608
  339.9 12.0 %slice-start.2 = ((s8[12582912]{0:T(1024)(128)(4,1)}), s8[4194304]{0:T(1024)(128)(4,1)S(1)}, s32[]{:S(2)}) async-start(s8[12582912]{0:T(1024)(128)(4,1)} %bitcast.112), calls=%async_computation.5 | async-start | bytes 8388608
  422.6 3.4 copy-start.4
  423.5 81.8 %collective-permute-start.4 = (f32[64,128]{1,0:T(8,128)S(1)}, f32[64,128]{1,0:T(8,128)S(1)}, u32[]{:S(2)}, u32[]{:S(2)}) collective-permute-start(f32[64,128]{1,0:T(8,128)S(1)} %get-tuple-element.6), channel_id=1, source_target_pairs={{0,1},{1,2},{2,3},{3,4},{4,5},{5,6},{6,7},{7,8},{8,9},{9,10},{10,1... | collective-permute-start | bytes 98312 | tf_op jit(solution)/shard_map/ppermute | solution.py:28
  424.7 80.5 %collective-permute-start.5 = (f32[64,128]{1,0:T(8,128)S(1)}, f32[64,128]{1,0:T(8,128)S(1)}, u32[]{:S(2)}, u32[]{:S(2)}) collective-permute-start(f32[64,128]{1,0:T(8,128)S(1)} %get-tuple-element.7), channel_id=1, source_target_pairs={{1,0},{2,1},{3,2},{4,3},{5,4},{6,5},{7,6},{8,7},{9,8},{10,9},{11,1... | collective-permute-start | bytes 98312 | tf_op jit(solution)/shard_map/ppermute | solution.py:31
  426.2 78.8 %copy-start.3 = (f32[4,8192]{1,0:T(4,128)S(1)}, f32[4,8192]{1,0:T(4,128)}, u32[]{:S(2)}) copy-start(f32[4,8192]{1,0:T(4,128)} %param.29) | copy-start | bytes 393220
  498.4 71.8 %all-to-all-start.1 = ((f32[16,512,128]{2,1,0:T(8,128)}), f32[16,512,128]{2,1,0:T(8,128)}, u32[]{:S(2)}, u32[]{:S(2)}) async-start(f32[16,512,128]{2,1,0:T(8,128)} %all-reduce.2.cloned.1.call-done), calls=%async_computation.1 | async-start | bytes 8388608 | tf_op jit(solution)/shard_map/all_to_all | solution.py:133
  513.0 20.2 %copy-start.1 = (f32[32,128,128]{2,0,1:T(8,128)S(1)}, f32[32,128,128]{2,0,1:T(8,128)}, u32[]{:S(2)}) copy-start(f32[32,128,128]{2,0,1:T(8,128)} %get-tuple-element.3) | copy-start | bytes 6291460
  580.0 6.3 %copy-start = (f32[8192,128]{1,0:T(8,128)S(1)}, f32[8192,128]{1,0:T(8,128)}, u32[]{:S(2)}) copy-start(f32[8192,128]{1,0:T(8,128)} %param.22) | copy-start | bytes 12582916
  580.0 6.3 %copy-start.2 = (f32[64,128,128]{2,1,0:T(8,128)S(1)}, f32[64,128,128]{2,1,0:T(8,128)}, u32[]{:S(2)}) copy-start(f32[64,128,128]{2,1,0:T(8,128)} %fusion.14) | copy-start | bytes 12582916
Sparse Core Ops, SparseCore 0:
  422.8 75.6 all-reduce.1
